TPU v7x, 512 devices: a whole 4x8x8 slice. The times are simulated.
512 devices in a mesh: seq: 16 (over z, core), head: 32 (over y, x).
Axes of the slice: x: 4, y: 8, z: 8, core: 2. Of those that a mesh axis runs over, the one named last changes fastest.
Arguments:
- queries: bfloat16 [65536, 4096], P(('seq', 'head')), may hold values from -6 to 6
- keys: bfloat16 [65536, 1024], P(('seq', 'head')), may hold values from -6 to 6
- values: bfloat16 [65536, 1024], P(('seq', 'head')), may hold values from -6 to 6
- out_grad: bfloat16 [65536, 4096], P(('seq', 'head')), may hold values from -6 to 6
Outputs:
- queries_grad: bfloat16 [65536, 4096], P(('seq', 'head'))
- keys_grad: bfloat16 [65536, 1024], P(('seq', 'head'))
- values_grad: bfloat16 [65536, 1024], P(('seq', 'head'))
All inputs are finite; a program needn't handle non-finite values.
Results may differ from a plain program's by a relative error of at most 0.0065.
Values may be sent and summed in bfloat16 or wider, within the bound.
A program may use at most 64 MiB of HBM per device.

v0:
```python
import jax
import jax.numpy as jnp
from jax import lax
from jax.sharding import PartitionSpec as P

HD = 128
BLK = 256


def carried_in(value, axis, join, neutral, backward):
    count, mine = (lax.axis_size(axis), lax.axis_index(axis))
    pieces = lax.all_gather(value, axis)
    if backward:
        pieces = pieces[::-1]
        mine = count - 1 - mine
    running = jnp.full_like(value, 0) + jnp.asarray(neutral, value.dtype)

    def step(position, running):
        longer = join(running, pieces[position])
        return jnp.where(position < mine, longer, running)

    return lax.fori_loop(0, count - 1, step, running)


def add_states(earlier, later):
    return earlier + later


def states_before(states):
    running = jnp.cumsum(states, axis=0)
    return jnp.concatenate([jnp.zeros_like(states[:1]), running[:-1]], axis=0)


def states_after(states):
    running = jnp.cumsum(states[::-1], axis=0)[::-1]
    return jnp.concatenate([running[1:], jnp.zeros_like(states[:1])], axis=0)


def block_grads(pieces):
    (
        query_block,
        key_block,
        value_block,
        cot_block,
        scaled_block,
        scale_block,
        prior_state,
        future_state,
    ) = pieces
    row_count = query_block.shape[0]
    causal = jnp.arange(row_count)[:, None] >= jnp.arange(row_count)[None, :]
    key_scores = jnp.einsum(
        "thd,shd->hts", query_block, key_block, preferred_element_type=jnp.float32
    )
    forward_weights = jnp.where(causal[None], scale_block[None, :, None] * key_scores, 0.0).astype(
        jnp.bfloat16
    )
    value_scores = jnp.einsum(
        "the,she->hts", scaled_block, value_block, preferred_element_type=jnp.float32
    )
    backward_weights = jnp.where(causal[None], value_scores, 0.0).astype(jnp.bfloat16)
    query_grad = jnp.einsum(
        "hts,shd->thd", backward_weights, key_block, preferred_element_type=jnp.float32
    )
    query_grad = query_grad + jnp.einsum(
        "the,hde->thd", scaled_block, prior_state, preferred_element_type=jnp.float32
    )
    key_grad = jnp.einsum(
        "hts,thd->shd", backward_weights, query_block, preferred_element_type=jnp.float32
    )
    key_grad = key_grad + jnp.einsum(
        "she,hed->shd", value_block, future_state, preferred_element_type=jnp.float32
    )
    value_grad = jnp.einsum(
        "hts,the->she", forward_weights, cot_block, preferred_element_type=jnp.float32
    )
    value_grad = value_grad + jnp.einsum(
        "shd,hed->she", key_block, future_state, preferred_element_type=jnp.float32
    )
    return (
        query_grad.astype(jnp.bfloat16),
        key_grad.astype(jnp.bfloat16),
        value_grad.astype(jnp.bfloat16),
    )


def seq_states(pair_total, grad_total):
    prior_group = carried_in(pair_total, "seq", add_states, jnp.zeros_like(pair_total), False)
    future_group = carried_in(grad_total, "seq", add_states, jnp.zeros_like(grad_total), True)
    return (prior_group, future_group)


def local_grads(query_local, key_local, value_local, cot_local, start, combine_states):
    local_tokens = query_local.shape[0]
    local_heads = query_local.shape[1]
    block_count = local_tokens // BLK
    positions = start + jnp.arange(local_tokens, dtype=jnp.int32)
    scale = 1.0 / jnp.sqrt((HD * (positions + 1)).astype(jnp.float32))
    scaled_cot = (scale[:, None, None] * cot_local.astype(jnp.float32)).astype(jnp.bfloat16)
    block_shape = (block_count, BLK, local_heads, HD)
    pair_shape = (block_count, BLK, 1, HD)
    query_blocks = query_local.reshape(block_shape)
    key_single = key_local.reshape(pair_shape)
    value_single = value_local.reshape(pair_shape)
    cot_blocks = cot_local.reshape(block_shape)
    scaled_blocks = scaled_cot.reshape(block_shape)
    pair_states = jnp.einsum(
        "bshd,bshe->bhde", key_single, value_single, preferred_element_type=jnp.float32
    )
    grad_states = jnp.einsum(
        "bthe,bthd->bhed", scaled_blocks, query_blocks, preferred_element_type=jnp.float32
    )
    prior_group, future_group = combine_states(
        jnp.sum(pair_states, axis=0), jnp.sum(grad_states, axis=0)
    )
    prior_states = prior_group[None] + states_before(pair_states)
    prior_states = prior_states.astype(jnp.bfloat16)
    future_states = (future_group[None] + states_after(grad_states)).astype(jnp.bfloat16)
    scale_blocks = scale.reshape(block_count, BLK)
    query_grad, key_grad, value_grad = lax.map(
        block_grads,
        (
            query_blocks,
            key_single,
            value_single,
            cot_blocks,
            scaled_blocks,
            scale_blocks,
            prior_states,
            future_states,
        ),
    )
    local_shape = (local_tokens, local_heads, HD)
    return (
        query_grad.reshape(local_shape),
        key_grad.reshape(local_shape),
        value_grad.reshape(local_shape),
    )


def body(queries, keys, values, out_grad):
    tok_dev = queries.shape[0]
    head_count = queries.shape[1] // HD
    kv_count = keys.shape[1] // HD
    group_size = head_count // kv_count
    seq_index = lax.axis_index("seq")
    query_cube = queries.reshape(tok_dev, head_count, HD)
    key_cube = jnp.repeat(keys.reshape(tok_dev, kv_count, HD), group_size, axis=1)
    value_cube = jnp.repeat(values.reshape(tok_dev, kv_count, HD), group_size, axis=1)
    cot_cube = out_grad.reshape(tok_dev, head_count, HD)
    query_local = lax.all_to_all(query_cube, "head", split_axis=1, concat_axis=0, tiled=True)
    key_local, value_local = (
        lax.all_to_all(key_cube, "head", split_axis=1, concat_axis=0, tiled=True),
        lax.all_to_all(value_cube, "head", split_axis=1, concat_axis=0, tiled=True),
    )
    cot_local = lax.all_to_all(cot_cube, "head", split_axis=1, concat_axis=0, tiled=True)
    local_tokens = query_local.shape[0]
    start = seq_index * local_tokens
    query_grad, key_grad, value_grad = local_grads(
        query_local, key_local, value_local, cot_local, start, seq_states
    )
    query_back, key_back, value_back = (
        lax.all_to_all(query_grad, "head", split_axis=0, concat_axis=1, tiled=True),
        lax.all_to_all(key_grad, "head", split_axis=0, concat_axis=1, tiled=True),
        lax.all_to_all(value_grad, "head", split_axis=0, concat_axis=1, tiled=True),
    )
    queries_grad = query_back.reshape(tok_dev, head_count * HD)
    key_sum = jnp.sum(
        key_back.reshape(tok_dev, kv_count, group_size, HD).astype(jnp.float32), axis=2
    )
    value_sum = jnp.sum(
        value_back.reshape(tok_dev, kv_count, group_size, HD).astype(jnp.float32), axis=2
    )
    keys_grad = key_sum.astype(jnp.bfloat16).reshape(tok_dev, kv_count * HD)
    values_grad = value_sum.astype(jnp.bfloat16).reshape(tok_dev, kv_count * HD)
    return (queries_grad, keys_grad, values_grad)


def solution(mesh):
    return jax.shard_map(
        body,
        mesh=mesh,
        in_specs=(
            P(("seq", "head"), None),
            P(("seq", "head"), None),
            P(("seq", "head"), None),
            P(("seq", "head"), None),
        ),
        out_specs=(P(("seq", "head"), None), P(("seq", "head"), None), P(("seq", "head"), None)),
        check_vma=False,
    )
```

profile of v0, /device:TPU:2, one launch (start us, length us, event | category | flops | bytes accessed | tf_op | source)
XLA Modules:
  0.0 489.5 jit_solution(16274256747867973477)
XLA Ops:
  7.2 2.4 copy.75
  9.6 10.2 %all-to-all-start.1 = ((bf16[128,32,128]{0,2,1:T(8,128)(2,1)}), bf16[128,32,128]{0,2,1:T(8,128)(2,1)S(1)}, u32[]{:S(2)}, u32[]{:S(2)}) async-start(bf16[128,32,128]{0,2,1:T(8,128)(2,1)} %bitcast.22), calls=%async_computation.1 | async-start | bytes 2097152 | tf_op jit(solution)/shard_map/all_to_all | solution.py:156
  21.1 26.8 %all-to-all-done.1 = bf16[128,32,128]{0,2,1:T(8,128)(2,1)S(1)} async-done(((bf16[128,32,128]{0,2,1:T(8,128)(2,1)}), bf16[128,32,128]{0,2,1:T(8,128)(2,1)S(1)}, u32[]{:S(2)}, u32[]{:S(2)}) %all-to-all-start.1) | async-done | bytes 1048608 | tf_op jit(solution)/shard_map/all_to_all | solution.py:156
  47.9 5.6 %all-to-all-start.3 = ((bf16[128,32,128]{0,2,1:T(8,128)(2,1)}), bf16[128,32,128]{0,2,1:T(8,128)(2,1)S(1)}, u32[]{:S(2)}, u32[]{:S(2)}) async-start(bf16[128,32,128]{0,2,1:T(8,128)(2,1)} %bitcast.40), calls=%async_computation.3 | async-start | bytes 2097152 | tf_op jit(solution)/shard_map/all_to_all | solution.py:151
  53.5 26.9 %all-to-all-done.3 = bf16[128,32,128]{0,2,1:T(8,128)(2,1)S(1)} async-done(((bf16[128,32,128]{0,2,1:T(8,128)(2,1)}), bf16[128,32,128]{0,2,1:T(8,128)(2,1)S(1)}, u32[]{:S(2)}, u32[]{:S(2)}) %all-to-all-start.3) | async-done | bytes 1048608 | tf_op jit(solution)/shard_map/all_to_all | solution.py:151
  81.8 5.6 %all-to-all-start = ((bf16[128,32,128]{2,0,1:T(8,128)(2,1)}), bf16[128,32,128]{2,0,1:T(8,128)(2,1)S(1)}, u32[]{:S(2)}, u32[]{:S(2)}) async-start(bf16[128,32,128]{2,0,1:T(8,128)(2,1)} %bitcast.17), calls=%async_computation | async-start | bytes 2097152 | tf_op jit(solution)/shard_map/all_to_all | solution.py:153
  87.4 26.5 %all-to-all-done = bf16[128,32,128]{2,0,1:T(8,128)(2,1)S(1)} async-done(((bf16[128,32,128]{2,0,1:T(8,128)(2,1)}), bf16[128,32,128]{2,0,1:T(8,128)(2,1)S(1)}, u32[]{:S(2)}, u32[]{:S(2)}) %all-to-all-start) | async-done | bytes 1048608 | tf_op jit(solution)/shard_map/all_to_all | solution.py:153
  115.2 5.6 %all-to-all-start.2 = ((bf16[128,32,128]{2,0,1:T(8,128)(2,1)}), bf16[128,32,128]{2,0,1:T(8,128)(2,1)}, u32[]{:S(2)}, u32[]{:S(2)}) async-start(bf16[128,32,128]{2,0,1:T(8,128)(2,1)} %bitcast.27), calls=%async_computation.2 | async-start | bytes 2097152 | tf_op jit(solution)/shard_map/all_to_all | solution.py:154
  122.5 1.9 copy.82
  124.4 2.3 copy.81
  126.7 4.2 fusion.63
  132.3 1.6 fusion.57
  135.0 2.2 slice.11
  137.3 9.9 %all-to-all-done.2 = bf16[128,32,128]{2,0,1:T(8,128)(2,1)} async-done(((bf16[128,32,128]{2,0,1:T(8,128)(2,1)}), bf16[128,32,128]{2,0,1:T(8,128)(2,1)}, u32[]{:S(2)}, u32[]{:S(2)}) %all-to-all-start.2) | async-done | bytes 1048608 | tf_op jit(solution)/shard_map/all_to_all | solution.py:154
  147.1 2.3 fusion.62
  154.2 22.9 %all-gather.7.cloned.1.call-done = f32[2048,128]{1,0:T(8,128)} async-done(((f32[128,128]{1,0:T(8,128)}), f32[2048,128]{1,0:T(8,128)}) %all-gather.7.cloned.1.call-update) | async-done | bytes 1048592 | tf_op jit(solution)/shard_map/all_gather | solution.py:12
  177.2 2.4 rev.7
  179.6 13.3 %while.44 = (s32[]{:T(128)}, f32[1,128,128]{2,1,0:T(8,128)S(1)}, s32[]{:T(128)}, f32[16,1,128,128]{3,2,1,0:T(8,128)}, s32[]{:T(128)}, /*index=5*/s32[]{:T(128)}) while((s32[]{:T(128)}, f32[1,128,128]{2,1,0:T(8,128)S(1)}, s32[]{:T(128)}, f32[16,1,128,128]{3,2,1,0:T(8,128)}, s32[]{:T(128)}, /*index=5*/s32[]{:T(128)}) %tuple.91), condition=%wide.region_6.7_spmd.clone, body=%wide.region_5.6_spmd.clone.sunk | while | flops 49156 | bytes 196701 | solution.py:22
  192.9 27.1 %all-gather.5.cloned.1.call-done = f32[2048,128]{1,0:T(8,128)} async-done(((f32[128,128]{1,0:T(8,128)}), f32[2048,128]{1,0:T(8,128)}) %all-gather.5.cloned.1.call-update) | async-done | bytes 1048592 | tf_op jit(solution)/shard_map/all_gather | solution.py:12
  220.0 13.2 %while.43 = (s32[]{:T(128)}, f32[1,128,128]{2,1,0:T(8,128)S(1)}, s32[]{:T(128)}, f32[16,1,128,128]{3,2,1,0:T(8,128)}, s32[]{:T(128)}, /*index=5*/s32[]{:T(128)}) while((s32[]{:T(128)}, f32[1,128,128]{2,1,0:T(8,128)S(1)}, s32[]{:T(128)}, f32[16,1,128,128]{3,2,1,0:T(8,128)}, s32[]{:T(128)}, /*index=5*/s32[]{:T(128)}) %tuple.104), condition=%wide.region_2.3_spmd.clone, body=%wide.region_1.0_spmd.clone.sunk | while | flops 49156 | bytes 196701 | solution.py:22
  233.2 2.1 add_convert_fusion
  236.3 131.7 %while.42 = (s32[]{:T(128)}, bf16[16,256,1,128]{3,1,0,2:T(8,128)(2,1)}, bf16[16,256,1,128]{3,1,0,2:T(8,128)(2,1)}, bf16[16,256,1,128]{3,1,0,2:T(8,128)(2,1)}, bf...) while((s32[]{:T(128)}, ...), condition=%wide.region_9.10_spmd, body=%wide.region_8.9_spmd.sunk | while | flops 109707264 | bytes 2926725 | solution.py:120
  368.5 2.7 reduce.6
  372.3 9.9 %all-to-all-start.4 = ((bf16[32,2,8192]{2,1,0:T(2,128)(2,1)}), bf16[32,2,8192]{2,1,0:T(2,128)(2,1)S(1)}, u32[]{:S(2)}, u32[]{:S(2)}) async-start(bf16[32,2,8192]{2,1,0:T(2,128)(2,1)} %reshape.234), calls=%async_computation.4 | async-start | bytes 2097152 | tf_op jit(solution)/shard_map/all_to_all | solution.py:163
  384.8 25.9 %all-to-all-done.4 = bf16[32,2,8192]{2,1,0:T(2,128)(2,1)S(1)} async-done(((bf16[32,2,8192]{2,1,0:T(2,128)(2,1)}), bf16[32,2,8192]{2,1,0:T(2,128)(2,1)S(1)}, u32[]{:S(2)}, u32[]{:S(2)}) %all-to-all-start.4) | async-done | bytes 1048608 | tf_op jit(solution)/shard_map/all_to_all | solution.py:163
  410.6 5.6 %all-to-all-start.5 = ((bf16[32,2,8192]{2,1,0:T(2,128)(2,1)}), bf16[32,2,8192]{2,1,0:T(2,128)(2,1)S(1)}, u32[]{:S(2)}, u32[]{:S(2)}) async-start(bf16[32,2,8192]{2,1,0:T(2,128)(2,1)} %reshape.236), calls=%async_computation.5 | async-start | bytes 2097152 | tf_op jit(solution)/shard_map/all_to_all | solution.py:164
  416.2 2.7 reduce.8
  420.0 23.6 %all-to-all-done.5 = bf16[32,2,8192]{2,1,0:T(2,128)(2,1)S(1)} async-done(((bf16[32,2,8192]{2,1,0:T(2,128)(2,1)}), bf16[32,2,8192]{2,1,0:T(2,128)(2,1)S(1)}, u32[]{:S(2)}, u32[]{:S(2)}) %all-to-all-start.5) | async-done | bytes 1048608 | tf_op jit(solution)/shard_map/all_to_all | solution.py:164
  444.6 5.6 %all-to-all-start.6 = ((bf16[32,2,8192]{2,1,0:T(2,128)(2,1)}), bf16[32,2,8192]{2,1,0:T(2,128)(2,1)}, u32[]{:S(2)}, u32[]{:S(2)}) async-start(bf16[32,2,8192]{2,1,0:T(2,128)(2,1)} %reshape.238), calls=%async_computation.6 | async-start | bytes 2097152 | tf_op jit(solution)/shard_map/all_to_all | solution.py:165
  452.4 1.7 copy.93
  457.8 19.2 %all-to-all-done.6 = bf16[32,2,8192]{2,1,0:T(2,128)(2,1)} async-done(((bf16[32,2,8192]{2,1,0:T(2,128)(2,1)}), bf16[32,2,8192]{2,1,0:T(2,128)(2,1)}, u32[]{:S(2)}, u32[]{:S(2)}) %all-to-all-start.6) | async-done | bytes 1048608 | tf_op jit(solution)/shard_map/all_to_all | solution.py:165
  477.0 4.3 reshape.239
  (299 shorter events, 184.0 us)
Async XLA Ops:
  7.2 46.3 %copy-start = (bf16[128,1024]{1,0:T(8,128)(2,1)S(1)}, bf16[128,1024]{1,0:T(8,128)(2,1)}, u32[]{:S(2)}) copy-start(bf16[128,1024]{1,0:T(8,128)(2,1)} %param.11) | copy-start | bytes 786436
  7.2 12.6 %copy-start.8 = (bf16[128,4096]{1,0:T(8,128)(2,1)S(1)}, bf16[128,4096]{1,0:T(8,128)(2,1)}, u32[]{:S(2)}) copy-start(bf16[128,4096]{1,0:T(8,128)(2,1)} %param.10) | copy-start | bytes 3145732
  9.6 38.3 %all-to-all-start.1 = ((bf16[128,32,128]{0,2,1:T(8,128)(2,1)}), bf16[128,32,128]{0,2,1:T(8,128)(2,1)S(1)}, u32[]{:S(2)}, u32[]{:S(2)}) async-start(bf16[128,32,128]{0,2,1:T(8,128)(2,1)} %bitcast.22), calls=%async_computation.1 | async-start | bytes 2097152 | tf_op jit(solution)/shard_map/all_to_all | solution.py:156
  47.9 32.6 %all-to-all-start.3 = ((bf16[128,32,128]{0,2,1:T(8,128)(2,1)}), bf16[128,32,128]{0,2,1:T(8,128)(2,1)S(1)}, u32[]{:S(2)}, u32[]{:S(2)}) async-start(bf16[128,32,128]{0,2,1:T(8,128)(2,1)} %bitcast.40), calls=%async_computation.3 | async-start | bytes 2097152 | tf_op jit(solution)/shard_map/all_to_all | solution.py:151
  53.5 33.9 %copy-start.9 = (bf16[128,1024]{1,0:T(8,128)(2,1)S(1)}, bf16[128,1024]{1,0:T(8,128)(2,1)}, u32[]{:S(2)}) copy-start(bf16[128,1024]{1,0:T(8,128)(2,1)} %param.12) | copy-start | bytes 786436
  80.5 1.3 copy-start.5
  81.8 32.1 %all-to-all-start = ((bf16[128,32,128]{2,0,1:T(8,128)(2,1)}), bf16[128,32,128]{2,0,1:T(8,128)(2,1)S(1)}, u32[]{:S(2)}, u32[]{:S(2)}) async-start(bf16[128,32,128]{2,0,1:T(8,128)(2,1)} %bitcast.17), calls=%async_computation | async-start | bytes 2097152 | tf_op jit(solution)/shard_map/all_to_all | solution.py:153
  113.9 7.1 %copy-start.1 = (bf16[128,32,128]{2,0,1:T(8,128)(2,1)}, bf16[128,32,128]{2,0,1:T(8,128)(2,1)S(1)}, u32[]{:S(2)}) copy-start(bf16[128,32,128]{2,0,1:T(8,128)(2,1)S(1)} %all-to-all-done) | copy-start | bytes 3145732
  115.2 31.9 %all-to-all-start.2 = ((bf16[128,32,128]{2,0,1:T(8,128)(2,1)}), bf16[128,32,128]{2,0,1:T(8,128)(2,1)}, u32[]{:S(2)}, u32[]{:S(2)}) async-start(bf16[128,32,128]{2,0,1:T(8,128)(2,1)} %bitcast.27), calls=%async_computation.2 | async-start | bytes 2097152 | tf_op jit(solution)/shard_map/all_to_all | solution.py:154
  120.9 56.3 %all-gather.7.cloned.1.call-start = ((), (), s32[]{:S(2)}) async-start(), calls=%async_computation.8 | async-start | bytes 1114112 | tf_op jit(solution)/shard_map/all_gather | solution.py:12
  130.9 89.1 %all-gather.5.cloned.1.call-start = ((), (), s32[]{:S(2)}) async-start(), calls=%async_computation.7 | async-start | bytes 1114112 | tf_op jit(solution)/shard_map/all_gather | solution.py:12
  133.9 13.2 %copy-start.2 = (bf16[128,32,128]{2,0,1:T(8,128)(2,1)S(1)}, bf16[128,32,128]{2,0,1:T(8,128)(2,1)}, u32[]{:S(2)}) copy-start(bf16[128,32,128]{2,0,1:T(8,128)(2,1)} %copy-done.1) | copy-start | bytes 3145732
  151.1 1.0 copy-start.6
  179.6 55.8 %slice-start = ((f32[16,1,128,128]{3,2,1,0:T(8,128)}), f32[15,1,128,128]{3,2,1,0:T(8,128)S(1)}, s32[]{:S(2)}) async-start(f32[16,1,128,128]{3,2,1,0:T(8,128)} %copy-done.6), calls=%async_computation.9 | async-start | bytes 1966080 | tf_op jit(solution)/shard_map/slice | solution.py:31
  371.2 11.0 %copy-start.7 = (bf16[16,256,1,128]{3,1,0,2:T(8,128)(2,1)S(1)}, bf16[16,256,1,128]{3,1,0,2:T(8,128)(2,1)}, u32[]{:S(2)}) copy-start(bf16[16,256,1,128]{3,1,0,2:T(8,128)(2,1)} %get-tuple-element.228) | copy-start | bytes 3145732
  372.3 38.4 %all-to-all-start.4 = ((bf16[32,2,8192]{2,1,0:T(2,128)(2,1)}), bf16[32,2,8192]{2,1,0:T(2,128)(2,1)S(1)}, u32[]{:S(2)}, u32[]{:S(2)}) async-start(bf16[32,2,8192]{2,1,0:T(2,128)(2,1)} %reshape.234), calls=%async_computation.4 | async-start | bytes 2097152 | tf_op jit(solution)/shard_map/all_to_all | solution.py:163
  410.6 33.0 %all-to-all-start.5 = ((bf16[32,2,8192]{2,1,0:T(2,128)(2,1)}), bf16[32,2,8192]{2,1,0:T(2,128)(2,1)S(1)}, u32[]{:S(2)}, u32[]{:S(2)}) async-start(bf16[32,2,8192]{2,1,0:T(2,128)(2,1)} %reshape.236), calls=%async_computation.5 | async-start | bytes 2097152 | tf_op jit(solution)/shard_map/all_to_all | solution.py:164
  443.6 1.0 copy-start.3
  444.6 32.4 %all-to-all-start.6 = ((bf16[32,2,8192]{2,1,0:T(2,128)(2,1)}), bf16[32,2,8192]{2,1,0:T(2,128)(2,1)}, u32[]{:S(2)}, u32[]{:S(2)}) async-start(bf16[32,2,8192]{2,1,0:T(2,128)(2,1)} %reshape.238), calls=%async_computation.6 | async-start | bytes 2097152 | tf_op jit(solution)/shard_map/all_to_all | solution.py:165
  452.4 3.0 copy-start.4
Sparse Core Ops, SparseCore 0:
  131.0 46.1 all-gather.6
  179.9 40.0 all-gather.4
where the time goes:
time: 497 us; the launch traced here: 490 us
  waiting for transfers between devices  209 us (42%)
  matrix products  111 us (22%)
  local copies, waits for them, and re-layouts  63.6 us (13%)
  starting transfers between devices  48.1 us (10%)
  other arithmetic  42.4 us (9%)
  between operations  14.4 us (3%)
    all_gather x2, waiting for transfers between devices, carried_in(): pieces = lax.all_gather(value, axis)  50 us
    all_to_all x1, waiting for transfers between devices, body(): lax.all_to_all(query_cube, 'head', split_axis=1, concat_axis=0, tiled=True)  26.9 us
    all_to_all x1, waiting for transfers between devices, body(): lax.all_to_all(cot_cube, 'head', split_axis=1, concat_axis=0, tiled=True)  26.8 us
    all_to_all x1, waiting for transfers between devices, body(): lax.all_to_all(key_cube, 'head', split_axis=1, concat_axis=0, tiled=True)  26.5 us
    dynamic_update_slice x80, local copies, waits for them, and re-layouts, local_grads(): lax.map(block_grads, (query_blocks, key_single, value_single, cot_blocks,...  26.4 us
    select_n x30, other arithmetic, step(): return jnp.where(position < mine, longer, running)  25.9 us
    all_to_all x1, waiting for transfers between devices, body(): lax.all_to_all(query_grad, 'head', split_axis=0, concat_axis=1, tiled=True)  25.9 us
    all_to_all x1, waiting for transfers between devices, body(): lax.all_to_all(key_grad, 'head', split_axis=0, concat_axis=1, tiled=True)  23.6 us
  transfers between devices with their start and end apart: 9, of which 9 were waited for; matrix products, arithmetic and copies ran while one was open for 11% of the time, Pallas kernels for 0%

commit v1 on v0

v1 whole, which is shorter than its diff:
```python
import functools

import jax
import jax.numpy as jnp
from jax import lax
from jax.experimental import pallas as pl
from jax.experimental.pallas import tpu as pltpu
from jax.sharding import PartitionSpec as P

HD = 128
GROUP = 4
KV = 8
RING_X = 4
SUB = 2
MESH = pl.DeviceIdType.MESH
F32 = jnp.float32
BF16 = jnp.bfloat16


def dot(left, right, left_dim, right_dim):
    return lax.dot_general(
        left, right, (((left_dim,), (right_dim,)), ((), ())), preferred_element_type=F32
    )


def kernel(
    nx, ny, nw,
    q_hbm, k_hbm, v_hbm, o_hbm, dq, dk, dv,
    q, k, v, o, s, dq_sum, dk_sum, dv_sum,
    x_out, x_in, y_out, y_in, z_out, z_in, yb_out, yb_in, xb_out, state,
    load_sem, send_sem, recv_sem, z_send, z_recv,
):
    w = lax.axis_index("seq")
    head = lax.axis_index("head")
    y, x = head // nx, head % nx
    mats = KV // nx // SUB
    rows = HD // ny
    tokens = q_hbm.shape[0]

    barrier = pltpu.get_barrier_semaphore()

    def greet(seq_to, head_to):
        pl.semaphore_signal(barrier, inc=1, device_id=(seq_to, head_to), device_id_type=MESH)

    for d in range(1, nx):
        greet(w, y * nx + (x + d) % nx)
    for d in range(1, ny):
        greet(w, (y + d) % ny * nx + x)

    @pl.loop(1, nw)
    def _(d):
        greet((w + d) % nw, head)

    loads = [
        pltpu.make_async_copy(src, dst, load_sem.at[i])
        for i, (src, dst) in enumerate(((k_hbm, k), (v_hbm, v), (o_hbm, o), (q_hbm, q)))
    ]
    for load in loads:
        load.start()

    first = (w * nx * ny + head) * tokens + 1

    def scale_along(axis):
        place = first + lax.broadcasted_iota(jnp.int32, (tokens, HD), axis)
        return 1.0 / jnp.sqrt((HD * place).astype(F32))

    def chunk(kind, sub):
        return kind * SUB + sub

    def remote(src, dst, stage, c, seq_to, head_to):
        return pltpu.make_async_remote_copy(
            src_ref=src, dst_ref=dst, send_sem=send_sem.at[stage, c], recv_sem=recv_sem.at[stage, c],
            device_id=(seq_to, head_to), device_id_type=MESH,
        )

    def all_x(src, dst, stage, kind, sub):
        return remote(
            src.at[kind, sub, pl.ds(0, nx - 1)], dst.at[kind, sub, pl.ds(0, nx - 1)],
            stage, chunk(kind, sub), w, y * nx + (x + 1) % nx,
        )

    def all_y(src, dst, stage, kind, sub):
        return remote(
            src.at[kind, sub, pl.ds(0, ny - 1)], dst.at[kind, sub, pl.ds(0, ny - 1)],
            stage, chunk(kind, sub), w, (y + 1) % ny * nx + x,
        )

    def send_x(src, dst, stage, kind, sub):
        for d in range(1, nx):
            to = (x + d) % nx
            remote(
                src.at[kind, sub, to], dst.at[kind, sub, x], stage, chunk(kind, sub), w, y * nx + to
            ).start()
        dst[kind, sub, x] = src[kind, sub, x]

    def send_y(src, dst, stage, kind, sub):
        for d in range(1, ny):
            to = (y + d) % ny
            remote(
                src.at[kind, sub, to], dst.at[kind, sub, y], stage, chunk(kind, sub), w, to * nx + x
            ).start()
        dst[kind, sub, y] = src[kind, sub, y]

    def z_copy(kind, sub, to, origin):
        return pltpu.make_async_remote_copy(
            src_ref=z_out.at[kind, sub], dst_ref=z_in.at[kind, sub, origin],
            send_sem=z_send.at[sub, to], recv_sem=z_recv.at[sub, origin],
            device_id=(to, head), device_id_type=MESH,
        )

    def order(kind, count):
        return range(count) if kind == 0 else range(count - 1, -1, -1)

    def after_x(kind, sub):
        all_x(x_out, x_in, 0, kind, sub).wait_recv()
        total = x_in[kind, sub, 0].astype(F32)
        for i in range(1, nx):
            total = total + x_in[kind, sub, i].astype(F32)
        total = total.astype(BF16)
        for i in range(ny):
            y_out[kind, sub, i] = total[:, i * rows : (i + 1) * rows]
        send_y(y_out, y_in, 1, kind, sub)

    def after_y(kind, sub):
        all_y(y_out, y_in, 1, kind, sub).wait_recv()
        total = y_in[kind, sub, 0].astype(F32)
        for i in range(1, ny):
            total = total + y_in[kind, sub, i].astype(F32)
        z_out[kind, sub] = total.astype(BF16)
        low, high = (w + 1, nw) if kind == 0 else (0, w)

        @pl.loop(low, high)
        def _(to):
            z_copy(kind, sub, to, w).start()

    def after_z(kind, sub):
        low, high = (0, w) if kind == 0 else (w + 1, nw)

        @pl.loop(low, high)
        def _(origin):
            z_copy(kind, sub, origin, origin).wait_recv()

        def add(origin, total):
            return total + z_in[kind, sub, origin].astype(F32)

        running = lax.fori_loop(low, high, add, jnp.zeros((mats, rows, HD), F32))
        for i in order(kind, ny):
            yb_out[kind, sub, i] = running.astype(BF16)
            running = running + y_in[kind, sub, i].astype(F32)
        send_y(yb_out, yb_in, 2, kind, sub)

    def after_yb(kind, sub):
        all_y(yb_out, yb_in, 2, kind, sub).wait_recv()
        for i in range(ny):
            part = slice(i * rows, (i + 1) * rows)
            running = yb_in[kind, sub, i].astype(F32)
            for j in order(kind, nx):
                xb_out[kind, sub, j, :, part] = running.astype(BF16)
                running = running + x_in[kind, sub, j, :, part].astype(F32)
        send_x(xb_out, state, 3, kind, sub)

    def cols(index, count=1):
        return pl.ds(pl.multiple_of(index * HD, HD), count * HD)

    def each_group(step):
        @pl.loop(0, nx)
        def _(owner):
            for sub in range(SUB):
                for m in range(mats):
                    step(owner * (KV // nx) + sub * mats + m, owner, sub, m)

    loads[0].wait()
    loads[1].wait()

    def pair_state(g, owner, sub, m):
        x_out[0, sub, owner, m] = dot(k[:, cols(g)], v[:, cols(g)], 0, 0).astype(BF16)

    each_group(pair_state)
    pl.semaphore_wait(barrier, nx - 1 + ny - 1 + nw - 1)
    for sub in range(SUB):
        send_x(x_out, x_in, 0, 0, sub)

    scale_rows = scale_along(0)
    loads[2].wait()
    loads[3].wait()

    def stacked(ref, g):
        return jnp.concatenate([ref[:, cols(g * GROUP + i)] for i in range(GROUP)], axis=0)

    def grad_state(g, owner, sub, m):
        for i in range(GROUP):
            at = cols(g * GROUP + i)
            s[:, at] = (scale_rows * o[:, at].astype(F32)).astype(BF16)
        x_out[1, sub, owner, m] = dot(stacked(s, g), stacked(q, g), 0, 0).astype(BF16)

    each_group(grad_state)
    for sub in range(SUB):
        send_x(x_out, x_in, 0, 1, sub)
    for sub in range(SUB):
        after_x(0, sub)

    scale_cols = scale_along(1)
    row = lax.broadcasted_iota(jnp.int32, (tokens, tokens), 0)
    col = lax.broadcasted_iota(jnp.int32, (tokens, tokens), 1)

    def within(low, high):
        @pl.loop(low, high)
        def _(g):
            key, value = k[:, cols(g)], v[:, cols(g)]
            forward, backward = [], []
            for i in range(GROUP):
                at = cols(g * GROUP + i)
                weights = scale_cols * dot(key, q[:, at], 1, 1)
                forward.append(jnp.where(row <= col, weights, 0.0).astype(BF16))
                weights = dot(value, s[:, at], 1, 1)
                backward.append(jnp.where(row <= col, weights, 0.0).astype(BF16))
                weights = dot(s[:, at], value, 1, 1)
                weights = jnp.where(col <= row, weights, 0.0).astype(BF16)
                dq_sum[:, at] = dot(weights, key, 1, 0)
            dk_sum[:, cols(g)] = dot(jnp.concatenate(backward, axis=1), stacked(q, g), 1, 0)
            dv_sum[:, cols(g)] = dot(jnp.concatenate(forward, axis=1), stacked(o, g), 1, 0)

    within(0, 2)
    for sub in range(SUB):
        after_x(1, sub)
    for sub in range(SUB):
        after_y(0, sub)
    within(2, 4)
    for sub in range(SUB):
        after_y(1, sub)
    for sub in range(SUB):
        after_z(0, sub)
    within(4, 6)
    for sub in range(SUB):
        after_z(1, sub)
    for sub in range(SUB):
        after_yb(0, sub)
    within(6, 8)
    for sub in range(SUB):
        after_yb(1, sub)

    for sub in range(SUB):
        all_x(xb_out, state, 3, 0, sub).wait_recv()

    def finish_query(g, owner, sub, m):
        add = dot(stacked(s, g), state[0, sub, owner, m], 1, 1)
        for i in range(GROUP):
            at = cols(g * GROUP + i)
            dq[:, at] = (dq_sum[:, at] + add[i * tokens : (i + 1) * tokens]).astype(BF16)

    each_group(finish_query)
    for sub in range(SUB):
        all_x(xb_out, state, 3, 1, sub).wait_recv()

    def finish_pair(g, owner, sub, m):
        future = state[1, sub, owner, m]
        at = cols(g)
        dk[:, at] = (dk_sum[:, at] + dot(v[:, at], future, 1, 0)).astype(BF16)
        dv[:, at] = (dv_sum[:, at] + dot(k[:, at], future, 1, 1)).astype(BF16)

    each_group(finish_pair)

    for kind in range(2):
        for sub in range(SUB):
            all_x(x_out, x_in, 0, kind, sub).wait_send()
            all_y(y_out, y_in, 1, kind, sub).wait_send()
            all_y(yb_out, yb_in, 2, kind, sub).wait_send()
            all_x(xb_out, state, 3, kind, sub).wait_send()
            low, high = (w + 1, nw) if kind == 0 else (0, w)

            @pl.loop(low, high)
            def _(to):
                z_copy(kind, sub, to, w).wait_send()


def body(nx, ny, nw, queries, keys, values, out_grad):
    tokens = queries.shape[0]
    mats = KV // nx // SUB
    rows = HD // ny
    wide, narrow = (tokens, queries.shape[1]), (tokens, keys.shape[1])
    by_x = pltpu.VMEM((2, SUB, nx, mats, HD, HD), BF16)
    by_y = pltpu.VMEM((2, SUB, ny, mats, rows, HD), BF16)
    return pl.pallas_call(
        functools.partial(kernel, nx, ny, nw),
        out_shape=(
            pltpu.VMEM(wide, BF16),
            pltpu.VMEM(narrow, BF16),
            pltpu.VMEM(narrow, BF16),
        ),
        in_specs=[pl.BlockSpec(memory_space=pltpu.HBM)] * 4,
        out_specs=(pl.BlockSpec(memory_space=pltpu.VMEM),) * 3,
        scratch_shapes=[
            pltpu.VMEM(wide, BF16),
            pltpu.VMEM(narrow, BF16),
            pltpu.VMEM(narrow, BF16),
            pltpu.VMEM(wide, BF16),
            pltpu.VMEM(wide, BF16),
            pltpu.VMEM(wide, F32),
            pltpu.VMEM(narrow, F32),
            pltpu.VMEM(narrow, F32),
            by_x,
            by_x,
            by_y,
            by_y,
            pltpu.VMEM((2, SUB, mats, rows, HD), BF16),
            pltpu.VMEM((2, SUB, nw, mats, rows, HD), BF16),
            by_y,
            by_y,
            by_x,
            by_x,
            pltpu.SemaphoreType.DMA((4,)),
            pltpu.SemaphoreType.DMA((4, 2 * SUB)),
            pltpu.SemaphoreType.DMA((4, 2 * SUB)),
            pltpu.SemaphoreType.DMA((SUB, nw)),
            pltpu.SemaphoreType.DMA((SUB, nw)),
        ],
        compiler_params=pltpu.CompilerParams(
            collective_id=0, has_side_effects=True, vmem_limit_bytes=48 * 2**20
        ),
    )(*(pltpu.with_memory_space_constraint(a, pltpu.HBM) for a in (queries, keys, values, out_grad)))


def solution(mesh, nx=RING_X):
    nw, heads = mesh.shape["seq"], mesh.shape["head"]
    spec = P(("seq", "head"), None)
    return jax.shard_map(
        functools.partial(body, nx, heads // nx, nw),
        mesh=mesh,
        in_specs=(spec,) * 4,
        out_specs=(spec,) * 3,
        check_vma=False,
    )
```

time: 497 us -> 46.1 us (0.09)
  the two profiles are of different devices: /device:TPU:2 before, /device:TPU:1 now
where the time goes in v1:
time: 46.1 us; the launch traced here: 45.8 us
  Pallas kernels  42.8 us (93%)
  local copies, waits for them, and re-layouts  2.38 us (5%)
  between operations  0.64 us (1%)
    pallas_call x1, Pallas kernels, body(): pl.pallas_call(functools.partial(kernel, nx, ny, nw), out_shape=(pltpu.VM...  42.8 us
    unnamed x3, local copies, waits for them, and re-layouts  2.38 us

profile of v1, /device:TPU:1, one launch (start us, length us, event | category | flops | bytes accessed | tf_op | source)
XLA Modules:
  0.0 45.8 jit_solution(2548602165663308608)
XLA Ops:
  0.6 42.8 %shard_map.67 = (bf16[128,4096]{1,0:T(8,128)(2,1)S(1)}, bf16[128,1024]{1,0:T(8,128)(2,1)S(1)}, bf16[128,1024]{1,0:T(8,128)(2,1)S(1)}) custom-call(bf16[128,4096]{1,0:T(8,128)(2,1)} %q_hbm.1, bf16[128,1024]{1,0:T(8,128)(2,1)} %k_hbm.1, bf16[128,1024]{1,0:T(8,128)(2,1)} %v_hbm.1, bf16[128,4096]{1,0:T(8,128)(2,1)} %o_hbm.1), custom_call_target="tpu_custom_call" | custom-call | tf_op jit(solution)/shard_map/pallas_call | solution.py:283
  43.4 1.0 %copy.10 = bf16[128,4096]{1,0:T(8,128)(2,1)} copy(bf16[128,4096]{1,0:T(8,128)(2,1)S(1)} %get-tuple-element.3) | data formatting | bytes 2097152
  44.4 0.7 %copy.11 = bf16[128,1024]{1,0:T(8,128)(2,1)} copy(bf16[128,1024]{1,0:T(8,128)(2,1)S(1)} %get-tuple-element.4) | data formatting | bytes 524288
  45.1 0.7 %copy.12 = bf16[128,1024]{1,0:T(8,128)(2,1)} copy(bf16[128,1024]{1,0:T(8,128)(2,1)S(1)} %get-tuple-element.5) | data formatting | bytes 524288

commit v2 on v1

--- a/solution.py
+++ b/solution.py
@@ -17,6 +17,10 @@
 BF16 = jnp.bfloat16
 
 
+def far_first(count):
+    return sorted(range(1, count), key=lambda d: -min(d, count - d))
+
+
 def dot(left, right, left_dim, right_dim):
     return lax.dot_general(
         left, right, (((left_dim,), (right_dim,)), ((), ())), preferred_element_type=F32
@@ -28,7 +32,7 @@
     q_hbm, k_hbm, v_hbm, o_hbm, dq, dk, dv,
     q, k, v, o, s, dq_sum, dk_sum, dv_sum,
     x_out, x_in, y_out, y_in, z_out, z_in, yb_out, yb_in, xb_out, state,
-    load_sem, send_sem, recv_sem, z_send, z_recv,
+    load_sem, send_sem, recv_sem, z_send, z_recv, here,
 ):
     w = lax.axis_index("seq")
     head = lax.axis_index("head")
@@ -42,18 +46,32 @@
     def greet(seq_to, head_to):
         pl.semaphore_signal(barrier, inc=1, device_id=(seq_to, head_to), device_id_type=MESH)
 
-    for d in range(1, nx):
+    for d in far_first(nx):
         greet(w, y * nx + (x + d) % nx)
-    for d in range(1, ny):
-        greet(w, (y + d) % ny * nx + x)
-
-    @pl.loop(1, nw)
-    def _(d):
-        greet((w + d) % nw, head)
+
+    def rank_of(place):
+        far = 2 * place // (ny + 1)
+        return (1 - far) * (2 * place - 1) + far * 2 * (ny - place) + (ny - place) // ny
+
+    rank = rank_of(y)
+
+    def each_column(step, above):
+        for d in far_first(ny):
+            other = (y + d) % ny
+
+            @pl.when(rank_of(other) > rank if above else rank_of(other) < rank)
+            def _():
+                step(w, other * nx + x)
+
+    each_column(greet, True)
+
+    @pl.loop(w + 1, nw)
+    def _(later_seq):
+        greet(later_seq, head)
 
     loads = [
         pltpu.make_async_copy(src, dst, load_sem.at[i])
-        for i, (src, dst) in enumerate(((k_hbm, k), (v_hbm, v), (o_hbm, o), (q_hbm, q)))
+        for i, (src, dst) in enumerate(((o_hbm, o), (q_hbm, q), (k_hbm, k), (v_hbm, v)))
     ]
     for load in loads:
         load.start()
@@ -86,7 +104,7 @@
         )
 
     def send_x(src, dst, stage, kind, sub):
-        for d in range(1, nx):
+        for d in far_first(nx):
             to = (x + d) % nx
             remote(
                 src.at[kind, sub, to], dst.at[kind, sub, x], stage, chunk(kind, sub), w, y * nx + to
@@ -94,7 +112,7 @@
         dst[kind, sub, x] = src[kind, sub, x]
 
     def send_y(src, dst, stage, kind, sub):
-        for d in range(1, ny):
+        for d in far_first(ny):
             to = (y + d) % ny
             remote(
                 src.at[kind, sub, to], dst.at[kind, sub, y], stage, chunk(kind, sub), w, to * nx + x
@@ -136,11 +154,8 @@
     def after_z(kind, sub):
         low, high = (0, w) if kind == 0 else (w + 1, nw)
 
-        @pl.loop(low, high)
-        def _(origin):
+        def add(origin, total):
             z_copy(kind, sub, origin, origin).wait_recv()
-
-        def add(origin, total):
             return total + z_in[kind, sub, origin].astype(F32)
 
         running = lax.fori_loop(low, high, add, jnp.zeros((mats, rows, HD), F32))
@@ -159,88 +174,93 @@
                 running = running + x_in[kind, sub, j, :, part].astype(F32)
         send_x(xb_out, state, 3, kind, sub)
 
-    def cols(index, count=1):
-        return pl.ds(pl.multiple_of(index * HD, HD), count * HD)
-
-    def each_group(step):
-        @pl.loop(0, nx)
-        def _(owner):
-            for sub in range(SUB):
+    def cols(index):
+        return slice(index * HD, (index + 1) * HD)
+
+    def each_group(step, subs=range(SUB)):
+        for sub in subs:
+            for owner in range(nx):
                 for m in range(mats):
                     step(owner * (KV // nx) + sub * mats + m, owner, sub, m)
 
+    def stacked(ref, g):
+        return jnp.concatenate([ref[:, cols(g * GROUP + i)] for i in range(GROUP)], axis=0)
+
+    scale_rows = scale_along(0)
     loads[0].wait()
     loads[1].wait()
 
+    def grad_state(g, owner, sub, m):
+        total = jnp.zeros((HD, HD), F32)
+        for i in range(GROUP):
+            at = cols(g * GROUP + i)
+            scaled = (scale_rows * o[:, at].astype(F32)).astype(BF16)
+            s[:, at] = scaled
+            total = total + dot(scaled, q[:, at], 0, 0)
+        x_out[1, sub, owner, m] = total.astype(BF16)
+
+    each_group(grad_state)
+    pl.semaphore_wait(barrier, nx - 1 + rank + w)
+    for sub in range(SUB):
+        send_x(x_out, x_in, 0, 1, sub)
+
+    def answer(seq_to, head_to, sem):
+        pl.semaphore_signal(sem, inc=1, device_id=(seq_to, head_to), device_id_type=MESH)
+
+    each_column(functools.partial(answer, sem=here.at[0]), False)
+
+    @pl.loop(0, w)
+    def _(earlier_seq):
+        answer(earlier_seq, head, here.at[1])
+
+    def await_answers(sem, count):
+        @pl.when(count > 0)
+        def _():
+            pl.semaphore_wait(sem, count)
+
+    loads[2].wait()
+    loads[3].wait()
+
     def pair_state(g, owner, sub, m):
         x_out[0, sub, owner, m] = dot(k[:, cols(g)], v[:, cols(g)], 0, 0).astype(BF16)
 
     each_group(pair_state)
-    pl.semaphore_wait(barrier, nx - 1 + ny - 1 + nw - 1)
     for sub in range(SUB):
         send_x(x_out, x_in, 0, 0, sub)
 
-    scale_rows = scale_along(0)
-    loads[2].wait()
-    loads[3].wait()
-
-    def stacked(ref, g):
-        return jnp.concatenate([ref[:, cols(g * GROUP + i)] for i in range(GROUP)], axis=0)
-
-    def grad_state(g, owner, sub, m):
-        for i in range(GROUP):
-            at = cols(g * GROUP + i)
-            s[:, at] = (scale_rows * o[:, at].astype(F32)).astype(BF16)
-        x_out[1, sub, owner, m] = dot(stacked(s, g), stacked(q, g), 0, 0).astype(BF16)
-
-    each_group(grad_state)
-    for sub in range(SUB):
-        send_x(x_out, x_in, 0, 1, sub)
-    for sub in range(SUB):
-        after_x(0, sub)
-
-    scale_cols = scale_along(1)
+    scale_cols = jnp.concatenate([scale_along(1)] * GROUP, axis=1)
     row = lax.broadcasted_iota(jnp.int32, (tokens, tokens), 0)
     col = lax.broadcasted_iota(jnp.int32, (tokens, tokens), 1)
-
-    def within(low, high):
-        @pl.loop(low, high)
-        def _(g):
-            key, value = k[:, cols(g)], v[:, cols(g)]
-            forward, backward = [], []
-            for i in range(GROUP):
-                at = cols(g * GROUP + i)
-                weights = scale_cols * dot(key, q[:, at], 1, 1)
-                forward.append(jnp.where(row <= col, weights, 0.0).astype(BF16))
-                weights = dot(value, s[:, at], 1, 1)
-                backward.append(jnp.where(row <= col, weights, 0.0).astype(BF16))
-                weights = dot(s[:, at], value, 1, 1)
-                weights = jnp.where(col <= row, weights, 0.0).astype(BF16)
-                dq_sum[:, at] = dot(weights, key, 1, 0)
-            dk_sum[:, cols(g)] = dot(jnp.concatenate(backward, axis=1), stacked(q, g), 1, 0)
-            dv_sum[:, cols(g)] = dot(jnp.concatenate(forward, axis=1), stacked(o, g), 1, 0)
-
-    within(0, 2)
-    for sub in range(SUB):
-        after_x(1, sub)
-    for sub in range(SUB):
-        after_y(0, sub)
-    within(2, 4)
-    for sub in range(SUB):
-        after_y(1, sub)
-    for sub in range(SUB):
-        after_z(0, sub)
-    within(4, 6)
-    for sub in range(SUB):
-        after_z(1, sub)
-    for sub in range(SUB):
-        after_yb(0, sub)
-    within(6, 8)
-    for sub in range(SUB):
-        after_yb(1, sub)
-
-    for sub in range(SUB):
-        all_x(xb_out, state, 3, 0, sub).wait_recv()
+    later = jnp.concatenate([row <= col] * GROUP, axis=1)
+    earlier = jnp.concatenate([col <= row] * GROUP, axis=0)
+
+    def within(g):
+        key, value = k[:, cols(g)], v[:, cols(g)]
+        query, scaled, cot = stacked(q, g), stacked(s, g), stacked(o, g)
+        forward = jnp.where(later, scale_cols * dot(key, query, 1, 1), 0.0).astype(BF16)
+        backward = jnp.where(later, dot(value, scaled, 1, 1), 0.0).astype(BF16)
+        weights = jnp.where(earlier, dot(scaled, value, 1, 1), 0.0).astype(BF16)
+        part = dot(weights, key, 1, 0)
+        for i in range(GROUP):
+            dq_sum[:, cols(g * GROUP + i)] = part[i * tokens : (i + 1) * tokens]
+        dk_sum[:, cols(g)] = dot(backward, query, 1, 0)
+        dv_sum[:, cols(g)] = dot(forward, cot, 1, 0)
+
+    for g in range(KV):
+        within(g)
+    def each_sub(step, kind):
+        for sub in range(SUB):
+            step(kind, sub)
+
+    await_answers(here.at[0], ny - 1 - rank)
+    each_sub(after_x, 1)
+    each_sub(after_x, 0)
+    each_sub(after_y, 1)
+    await_answers(here.at[1], nw - 1 - w)
+    each_sub(after_y, 0)
+    each_sub(after_z, 0)
+    each_sub(after_yb, 0)
+    each_sub(after_z, 1)
 
     def finish_query(g, owner, sub, m):
         add = dot(stacked(s, g), state[0, sub, owner, m], 1, 1)
@@ -248,17 +268,20 @@
             at = cols(g * GROUP + i)
             dq[:, at] = (dq_sum[:, at] + add[i * tokens : (i + 1) * tokens]).astype(BF16)
 
-    each_group(finish_query)
-    for sub in range(SUB):
-        all_x(xb_out, state, 3, 1, sub).wait_recv()
-
     def finish_pair(g, owner, sub, m):
         future = state[1, sub, owner, m]
         at = cols(g)
         dk[:, at] = (dk_sum[:, at] + dot(v[:, at], future, 1, 0)).astype(BF16)
         dv[:, at] = (dv_sum[:, at] + dot(k[:, at], future, 1, 1)).astype(BF16)
 
-    each_group(finish_pair)
+    def finish(kind, step):
+        for sub in range(SUB):
+            all_x(xb_out, state, 3, kind, sub).wait_recv()
+            each_group(step, (sub,))
+
+    finish(0, finish_query)
+    each_sub(after_yb, 1)
+    finish(1, finish_pair)
 
     for kind in range(2):
         for sub in range(SUB):
@@ -273,6 +296,18 @@
                 z_copy(kind, sub, to, w).wait_send()
 
 
+def write_back(*refs):
+    sources, results, sems = refs[:3], refs[3:6], refs[6]
+    copies = [
+        pltpu.make_async_copy(source, result, sems.at[i])
+        for i, (source, result) in enumerate(zip(sources, results))
+    ]
+    for copy in copies:
+        copy.start()
+    for copy in copies:
+        copy.wait()
+
+
 def body(nx, ny, nw, queries, keys, values, out_grad):
     tokens = queries.shape[0]
     mats = KV // nx // SUB
@@ -280,7 +315,7 @@
     wide, narrow = (tokens, queries.shape[1]), (tokens, keys.shape[1])
     by_x = pltpu.VMEM((2, SUB, nx, mats, HD, HD), BF16)
     by_y = pltpu.VMEM((2, SUB, ny, mats, rows, HD), BF16)
-    return pl.pallas_call(
+    grads = pl.pallas_call(
         functools.partial(kernel, nx, ny, nw),
         out_shape=(
             pltpu.VMEM(wide, BF16),
@@ -313,11 +348,20 @@
             pltpu.SemaphoreType.DMA((4, 2 * SUB)),
             pltpu.SemaphoreType.DMA((SUB, nw)),
             pltpu.SemaphoreType.DMA((SUB, nw)),
+            pltpu.SemaphoreType.REGULAR((2,)),
         ],
         compiler_params=pltpu.CompilerParams(
             collective_id=0, has_side_effects=True, vmem_limit_bytes=48 * 2**20
         ),
     )(*(pltpu.with_memory_space_constraint(a, pltpu.HBM) for a in (queries, keys, values, out_grad)))
+    return pl.pallas_call(
+        write_back,
+        out_shape=(pltpu.HBM(wide, BF16), pltpu.HBM(narrow, BF16), pltpu.HBM(narrow, BF16)),
+        in_specs=[pl.BlockSpec(memory_space=pltpu.VMEM)] * 3,
+        out_specs=(pl.BlockSpec(memory_space=pltpu.HBM),) * 3,
+        scratch_shapes=[pltpu.SemaphoreType.DMA((3,))],
+        compiler_params=pltpu.CompilerParams(vmem_limit_bytes=16 * 2**20),
+    )(*grads)
 
 
 def solution(mesh, nx=RING_X):

time: 46.1 us -> 39.4 us (0.85)
  Pallas kernels: 42.8 us -> 38.6 us
  local copies, waits for them, and re-layouts: 2.38 us -> 0 us
    pallas_call x1, Pallas kernels: 42.8 us -> 37.5 us  [body(): pl.pallas_call(functools.partial(kernel, nx, ny, nw), out_shape=(pltpu.VM...]
    unnamed x3 -> x0, local copies, waits for them, and re-layouts: 2.38 us -> none
    pallas_call x0 -> x1, Pallas kernels: none -> 1.16 us  [body(): pl.pallas_call(write_back, out_shape=(pltpu.HBM(wide, BF16), pltpu.HBM(na...]
where the time goes in v2:
time: 39.4 us; the launch traced here: 39.3 us
  Pallas kernels  38.6 us (98%)
  between operations  0.64 us (2%)
    pallas_call x1, Pallas kernels, body(): pl.pallas_call(functools.partial(kernel, nx, ny, nw), out_shape=(pltpu.VM...  37.5 us
    pallas_call x1, Pallas kernels, body(): pl.pallas_call(write_back, out_shape=(pltpu.HBM(wide, BF16), pltpu.HBM(na...  1.16 us

profile of v2, /device:TPU:1, one launch (start us, length us, event | category | flops | bytes accessed | tf_op | source)
XLA Modules:
  0.0 39.3 jit_solution(4807034568619659240)
XLA Ops:
  0.6 37.5 %shard_map.67 = (bf16[128,4096]{1,0:T(8,128)(2,1)S(1)}, bf16[128,1024]{1,0:T(8,128)(2,1)S(1)}, bf16[128,1024]{1,0:T(8,128)(2,1)S(1)}) custom-call(bf16[128,4096]{1,0:T(8,128)(2,1)} %q_hbm.1, bf16[128,1024]{1,0:T(8,128)(2,1)} %k_hbm.1, bf16[128,1024]{1,0:T(8,128)(2,1)} %v_hbm.1, bf16[128,4096]{1,0:T(8,128)(2,1)} %o_hbm.1), custom_call_target="tpu_custom_call" | custom-call | tf_op jit(solution)/shard_map/pallas_call | solution.py:318
  38.1 1.2 %shard_map.68 = (bf16[128,4096]{1,0:T(8,128)(2,1)}, bf16[128,1024]{1,0:T(8,128)(2,1)}, bf16[128,1024]{1,0:T(8,128)(2,1)}) custom-call(bf16[128,4096]{1,0:T(8,128)(2,1)S(1)} %get-tuple-element.6.refs_0_, bf16[128,1024]{1,0:T(8,128)(2,1)S(1)} %get-tuple-element.7.refs_1_, bf16[128,1024]{1,0:T(8,128)(2,1)S(1)} %get-tuple-element.8.refs_2_), custom_call_target="tpu_custom_call" | custom-call | tf_op jit(solution)/shard_map/pallas_call | solution.py:357

commit v3 on v2

--- a/solution.py
+++ b/solution.py
@@ -69,9 +69,19 @@
     def _(later_seq):
         greet(later_seq, head)
 
+    def half(sub):
+        return pl.ds(sub * (q.shape[1] // SUB), q.shape[1] // SUB)
+
     loads = [
         pltpu.make_async_copy(src, dst, load_sem.at[i])
-        for i, (src, dst) in enumerate(((o_hbm, o), (q_hbm, q), (k_hbm, k), (v_hbm, v)))
+        for i, (src, dst) in enumerate(
+            [
+                (ref_from.at[:, half(sub)], ref_to.at[:, half(sub)])
+                for sub in range(SUB)
+                for ref_from, ref_to in ((o_hbm, o), (q_hbm, q))
+            ]
+            + [(k_hbm, k), (v_hbm, v)]
+        )
     ]
     for load in loads:
         load.start()
@@ -139,14 +149,15 @@
             y_out[kind, sub, i] = total[:, i * rows : (i + 1) * rows]
         send_y(y_out, y_in, 1, kind, sub)
 
-    def after_y(kind, sub):
+    def after_y(kind, sub, end=nw):
         all_y(y_out, y_in, 1, kind, sub).wait_recv()
         total = y_in[kind, sub, 0].astype(F32)
         for i in range(1, ny):
             total = total + y_in[kind, sub, i].astype(F32)
         z_out[kind, sub] = total.astype(BF16)
-        low, high = (w + 1, nw) if kind == 0 else (0, w)
-
+        start_z(kind, sub, *((w + 1, end) if kind == 0 else (0, w)))
+
+    def start_z(kind, sub, low, high):
         @pl.loop(low, high)
         def _(to):
             z_copy(kind, sub, to, w).start()
@@ -181,14 +192,25 @@
         for sub in subs:
             for owner in range(nx):
                 for m in range(mats):
-                    step(owner * (KV // nx) + sub * mats + m, owner, sub, m)
+                    step(sub * (KV // SUB) + owner * mats + m, owner, sub, m)
 
     def stacked(ref, g):
         return jnp.concatenate([ref[:, cols(g * GROUP + i)] for i in range(GROUP)], axis=0)
 
+    pl.semaphore_wait(barrier, nx - 1 + rank + w)
+
+    def answer(seq_to, head_to, sem):
+        pl.semaphore_signal(sem, inc=1, device_id=(seq_to, head_to), device_id_type=MESH)
+
+    each_column(functools.partial(answer, sem=here.at[0]), False)
+
+    @pl.loop(0, w)
+    def _(earlier_seq):
+        answer(earlier_seq, head, here.at[1 + w // (nw // 2)])
+
+    early = w < nw // 2
+
     scale_rows = scale_along(0)
-    loads[0].wait()
-    loads[1].wait()
 
     def grad_state(g, owner, sub, m):
         total = jnp.zeros((HD, HD), F32)
@@ -199,34 +221,33 @@
             total = total + dot(scaled, q[:, at], 0, 0)
         x_out[1, sub, owner, m] = total.astype(BF16)
 
-    each_group(grad_state)
-    pl.semaphore_wait(barrier, nx - 1 + rank + w)
     for sub in range(SUB):
-        send_x(x_out, x_in, 0, 1, sub)
-
-    def answer(seq_to, head_to, sem):
-        pl.semaphore_signal(sem, inc=1, device_id=(seq_to, head_to), device_id_type=MESH)
-
-    each_column(functools.partial(answer, sem=here.at[0]), False)
-
-    @pl.loop(0, w)
-    def _(earlier_seq):
-        answer(earlier_seq, head, here.at[1])
+        loads[2 * sub].wait()
+        loads[2 * sub + 1].wait()
+        each_group(grad_state, (sub,))
+
+        @pl.when(jnp.logical_not(early))
+        def _():
+            send_x(x_out, x_in, 0, 1, sub)
 
     def await_answers(sem, count):
         @pl.when(count > 0)
         def _():
             pl.semaphore_wait(sem, count)
 
-    loads[2].wait()
-    loads[3].wait()
+    loads[-2].wait()
+    loads[-1].wait()
 
     def pair_state(g, owner, sub, m):
         x_out[0, sub, owner, m] = dot(k[:, cols(g)], v[:, cols(g)], 0, 0).astype(BF16)
 
     each_group(pair_state)
-    for sub in range(SUB):
-        send_x(x_out, x_in, 0, 0, sub)
+
+    @pl.when(early)
+    def _():
+        for kind in range(2):
+            for sub in range(SUB):
+                send_x(x_out, x_in, 0, kind, sub)
 
     scale_cols = jnp.concatenate([scale_along(1)] * GROUP, axis=1)
     row = lax.broadcasted_iota(jnp.int32, (tokens, tokens), 0)
@@ -248,19 +269,41 @@
 
     for g in range(KV):
         within(g)
+    @pl.when(jnp.logical_not(early))
+    def _():
+        for sub in range(SUB):
+            send_x(x_out, x_in, 0, 0, sub)
+
     def each_sub(step, kind):
         for sub in range(SUB):
             step(kind, sub)
 
     await_answers(here.at[0], ny - 1 - rank)
-    each_sub(after_x, 1)
-    each_sub(after_x, 0)
-    each_sub(after_y, 1)
-    await_answers(here.at[1], nw - 1 - w)
-    each_sub(after_y, 0)
-    each_sub(after_z, 0)
-    each_sub(after_yb, 0)
-    each_sub(after_z, 1)
+
+    @pl.when(early)
+    def _():
+        each_sub(after_x, 0)
+        each_sub(after_x, 1)
+        await_answers(here.at[1], nw // 2 - 1 - w)
+        each_sub(functools.partial(after_y, end=nw // 2), 0)
+        each_sub(after_y, 1)
+        each_sub(after_z, 0)
+        await_answers(here.at[2], nw // 2)
+        for sub in range(SUB):
+            start_z(0, sub, nw // 2, nw)
+        each_sub(after_yb, 0)
+        each_sub(after_z, 1)
+
+    @pl.when(jnp.logical_not(early))
+    def _():
+        each_sub(after_x, 1)
+        each_sub(after_x, 0)
+        each_sub(after_y, 1)
+        await_answers(here.at[2], nw - 1 - w)
+        each_sub(after_y, 0)
+        each_sub(after_z, 0)
+        each_sub(after_z, 1)
+        each_sub(after_yb, 0)
 
     def finish_query(g, owner, sub, m):
         add = dot(stacked(s, g), state[0, sub, owner, m], 1, 1)
@@ -279,8 +322,8 @@
             all_x(xb_out, state, 3, kind, sub).wait_recv()
             each_group(step, (sub,))
 
+    each_sub(after_yb, 1)
     finish(0, finish_query)
-    each_sub(after_yb, 1)
     finish(1, finish_pair)
 
     for kind in range(2):
@@ -343,12 +386,12 @@
             by_y,
             by_x,
             by_x,
-            pltpu.SemaphoreType.DMA((4,)),
+            pltpu.SemaphoreType.DMA((2 * SUB + 2,)),
             pltpu.SemaphoreType.DMA((4, 2 * SUB)),
             pltpu.SemaphoreType.DMA((4, 2 * SUB)),
             pltpu.SemaphoreType.DMA((SUB, nw)),
             pltpu.SemaphoreType.DMA((SUB, nw)),
-            pltpu.SemaphoreType.REGULAR((2,)),
+            pltpu.SemaphoreType.REGULAR((3,)),
         ],
         compiler_params=pltpu.CompilerParams(
             collective_id=0, has_side_effects=True, vmem_limit_bytes=48 * 2**20

time: 39.4 us -> 38.4 us (0.975)
  Pallas kernels: 38.6 us -> 37.6 us
    pallas_call x1, Pallas kernels: 37.5 us -> 36.4 us  [body(): pl.pallas_call(functools.partial(kernel, nx, ny, nw), out_shape=(pltpu.VM...]
where the time goes in v3:
time: 38.4 us; the launch traced here: 38.2 us
  Pallas kernels  37.6 us (98%)
  between operations  0.64 us (2%)
    pallas_call x1, Pallas kernels, body(): pl.pallas_call(functools.partial(kernel, nx, ny, nw), out_shape=(pltpu.VM...  36.4 us
    pallas_call x1, Pallas kernels, body(): pl.pallas_call(write_back, out_shape=(pltpu.HBM(wide, BF16), pltpu.HBM(na...  1.16 us

profile of v3, /device:TPU:1, one launch (start us, length us, event | category | flops | bytes accessed | tf_op | source)
XLA Modules:
  0.0 38.2 jit_solution(10105643361723074079)
XLA Ops:
  0.6 36.4 %shard_map.67 = (bf16[128,4096]{1,0:T(8,128)(2,1)S(1)}, bf16[128,1024]{1,0:T(8,128)(2,1)S(1)}, bf16[128,1024]{1,0:T(8,128)(2,1)S(1)}) custom-call(bf16[128,4096]{1,0:T(8,128)(2,1)} %q_hbm.1, bf16[128,1024]{1,0:T(8,128)(2,1)} %k_hbm.1, bf16[128,1024]{1,0:T(8,128)(2,1)} %v_hbm.1, bf16[128,4096]{1,0:T(8,128)(2,1)} %o_hbm.1), custom_call_target="tpu_custom_call" | custom-call | tf_op jit(solution)/shard_map/pallas_call | solution.py:361
  37.0 1.2 %shard_map.68 = (bf16[128,4096]{1,0:T(8,128)(2,1)}, bf16[128,1024]{1,0:T(8,128)(2,1)}, bf16[128,1024]{1,0:T(8,128)(2,1)}) custom-call(bf16[128,4096]{1,0:T(8,128)(2,1)S(1)} %get-tuple-element.6.refs_0_, bf16[128,1024]{1,0:T(8,128)(2,1)S(1)} %get-tuple-element.7.refs_1_, bf16[128,1024]{1,0:T(8,128)(2,1)S(1)} %get-tuple-element.8.refs_2_), custom_call_target="tpu_custom_call" | custom-call | tf_op jit(solution)/shard_map/pallas_call | solution.py:400

commit v4 on v3

--- a/solution.py
+++ b/solution.py
@@ -41,34 +41,6 @@
     rows = HD // ny
     tokens = q_hbm.shape[0]
 
-    barrier = pltpu.get_barrier_semaphore()
-
-    def greet(seq_to, head_to):
-        pl.semaphore_signal(barrier, inc=1, device_id=(seq_to, head_to), device_id_type=MESH)
-
-    for d in far_first(nx):
-        greet(w, y * nx + (x + d) % nx)
-
-    def rank_of(place):
-        far = 2 * place // (ny + 1)
-        return (1 - far) * (2 * place - 1) + far * 2 * (ny - place) + (ny - place) // ny
-
-    rank = rank_of(y)
-
-    def each_column(step, above):
-        for d in far_first(ny):
-            other = (y + d) % ny
-
-            @pl.when(rank_of(other) > rank if above else rank_of(other) < rank)
-            def _():
-                step(w, other * nx + x)
-
-    each_column(greet, True)
-
-    @pl.loop(w + 1, nw)
-    def _(later_seq):
-        greet(later_seq, head)
-
     def half(sub):
         return pl.ds(sub * (q.shape[1] // SUB), q.shape[1] // SUB)
 
@@ -86,6 +58,35 @@
     for load in loads:
         load.start()
 
+    barrier = pltpu.get_barrier_semaphore()
+
+    def greet(seq_to, head_to):
+        pl.semaphore_signal(barrier, inc=1, device_id=(seq_to, head_to), device_id_type=MESH)
+
+    for d in far_first(nx):
+        greet(w, y * nx + (x + d) % nx)
+
+    def rank_of(place):
+        far = 2 * place // (ny + 1)
+        return (1 - far) * (2 * place - 1) + far * 2 * (ny - place) + (ny - place) // ny
+
+    rank = rank_of(y)
+
+    def each_column(step, above):
+        for d in far_first(ny):
+            other = (y + d) % ny
+
+            @pl.when(rank_of(other) > rank if above else rank_of(other) < rank)
+            def _():
+                step(w, other * nx + x)
+
+    each_column(greet, True)
+
+    @pl.loop(w + 1, nw)
+    def _(later_seq):
+        greet(later_seq, head)
+
+
     first = (w * nx * ny + head) * tokens + 1
 
     def scale_along(axis):
@@ -245,9 +246,9 @@
 
     @pl.when(early)
     def _():
-        for kind in range(2):
-            for sub in range(SUB):
-                send_x(x_out, x_in, 0, kind, sub)
+        for sub in range(SUB):
+            send_x(x_out, x_in, 0, 0, sub)
+
 
     scale_cols = jnp.concatenate([scale_along(1)] * GROUP, axis=1)
     row = lax.broadcasted_iota(jnp.int32, (tokens, tokens), 0)
@@ -269,6 +270,12 @@
 
     for g in range(KV):
         within(g)
+
+    @pl.when(early)
+    def _():
+        for sub in range(SUB):
+            send_x(x_out, x_in, 0, 1, sub)
+
     @pl.when(jnp.logical_not(early))
     def _():
         for sub in range(SUB):
@@ -324,19 +331,21 @@
 
     each_sub(after_yb, 1)
     finish(0, finish_query)
-    finish(1, finish_pair)
-
     for kind in range(2):
         for sub in range(SUB):
             all_x(x_out, x_in, 0, kind, sub).wait_send()
             all_y(y_out, y_in, 1, kind, sub).wait_send()
             all_y(yb_out, yb_in, 2, kind, sub).wait_send()
-            all_x(xb_out, state, 3, kind, sub).wait_send()
             low, high = (w + 1, nw) if kind == 0 else (0, w)
 
             @pl.loop(low, high)
             def _(to):
                 z_copy(kind, sub, to, w).wait_send()
+    for sub in range(SUB):
+        all_x(xb_out, state, 3, 0, sub).wait_send()
+    finish(1, finish_pair)
+    for sub in range(SUB):
+        all_x(xb_out, state, 3, 1, sub).wait_send()
 
 
 def write_back(*refs):

time: 38.4 us -> 38.1 us (level)
  no operation moved by 1% of the time
where the time goes in v4:
time: 38.1 us; the launch traced here: 37.9 us
  Pallas kernels  37.3 us (98%)
  between operations  0.64 us (2%)
    pallas_call x1, Pallas kernels, body(): pl.pallas_call(functools.partial(kernel, nx, ny, nw), out_shape=(pltpu.VM...  36.1 us
    pallas_call x1, Pallas kernels, body(): pl.pallas_call(write_back, out_shape=(pltpu.HBM(wide, BF16), pltpu.HBM(na...  1.16 us

profile of v4, /device:TPU:1, one launch (start us, length us, event | category | flops | bytes accessed | tf_op | source)
XLA Modules:
  0.0 37.9 jit_solution(1531292288800712456)
XLA Ops:
  0.6 36.1 %shard_map.67 = (bf16[128,4096]{1,0:T(8,128)(2,1)S(1)}, bf16[128,1024]{1,0:T(8,128)(2,1)S(1)}, bf16[128,1024]{1,0:T(8,128)(2,1)S(1)}) custom-call(bf16[128,4096]{1,0:T(8,128)(2,1)} %q_hbm.1, bf16[128,1024]{1,0:T(8,128)(2,1)} %k_hbm.1, bf16[128,1024]{1,0:T(8,128)(2,1)} %v_hbm.1, bf16[128,4096]{1,0:T(8,128)(2,1)} %o_hbm.1), custom_call_target="tpu_custom_call" | custom-call | tf_op jit(solution)/shard_map/pallas_call | solution.py:370
  36.7 1.2 %shard_map.68 = (bf16[128,4096]{1,0:T(8,128)(2,1)}, bf16[128,1024]{1,0:T(8,128)(2,1)}, bf16[128,1024]{1,0:T(8,128)(2,1)}) custom-call(bf16[128,4096]{1,0:T(8,128)(2,1)S(1)} %get-tuple-element.6.refs_0_, bf16[128,1024]{1,0:T(8,128)(2,1)S(1)} %get-tuple-element.7.refs_1_, bf16[128,1024]{1,0:T(8,128)(2,1)S(1)} %get-tuple-element.8.refs_2_), custom_call_target="tpu_custom_call" | custom-call | tf_op jit(solution)/shard_map/pallas_call | solution.py:409
